TPU v7x, 32 devices: a whole 2x2x4 slice. The times are simulated.
32 devices in a mesh: groups: 2 (over y), seq: 4 (over x, core), heads: 4 (over z).
Axes of the slice: x: 2, y: 2, z: 4, core: 2. Of those that a mesh axis runs over, the one named last changes fastest.
Arguments:
- tokens: bfloat16 [4096, 8192], P(('groups', 'seq'), 'heads'), parts along dimension 0, may hold values from -6 to 6
- xz_weight: bfloat16 [8192, 32768], P(None, ('heads', 'seq')), may hold values from -0.0625 to 0.0625
- bc_weight: bfloat16 [8192, 2048], P(None, 'heads'), may hold values from -0.0625 to 0.0625
- step_weight: bfloat16 [8192, 256], P(None, 'heads'), may hold values from -0.0625 to 0.0625
- step_bias: float32 [256], P('heads'), may hold values from -4 to -2
- decay_log: float32 [256], P('heads'), may hold values from -5.3 to -0.7
- skip_gain: float32 [256], P('heads'), may hold values from 0.5 to 2
- conv_weight: float32 [4, 16384], P(None, 'heads'), may hold values from -3 to 3
- conv_bias: float32 [16384], P('heads'), may hold values from -3 to 3
- bc_conv_weight: float32 [4, 2048], replicated, may hold values from -3 to 3
- bc_conv_bias: float32 [2048], replicated, may hold values from -3 to 3
- norm_gain: float32 [16384], P('heads'), may hold values from 0.1 to 1.9
- step_bounds: int32 [32], P('groups'), parts along dimension 0, may hold values from 0 to 2047, as said below
- readers: int32 [32], P('groups'), parts along dimension 0, may hold values from 0 to 3, as said below
Outputs:
- mixed: bfloat16 [4096, 16384], P(('groups', 'seq'), 'heads'), parts along dimension 0
- handoff: bfloat16 [8, 4, 256, 64, 128], P(('groups', 'heads'), None, 'seq'), parts along dimension 0
There are 2 independent parts, one for each index of `groups`. A program takes and returns all parts, laid end to end along the dimension named above; an argument that names none is the same for every part. Nothing has to cross between parts.
Inputs may be any that keep to these rules, and one draw needn't show every extreme that they name: `step_bounds`: boundary j * 4 + i, for i < 4, lies in section j: positions j * 512 to (j + 1) * 512 - 1. The first boundary is at position 0 and the last at 2047. `readers`: among the 4 boundaries of each section every reader appears exactly once.
All inputs are finite; a program needn't handle non-finite values.
Results may differ from a plain program's by a relative error of at most 0.0056.
Values may be sent and summed in bfloat16 or wider, within the bound.
A program may use at most 384 MiB of HBM per device.

v0:
```python
import jax
import jax.numpy as jnp
from jax import lax
from jax.sharding import PartitionSpec as P

H = 256
P_SIZE = 64
N = 128
G = 8
CH = 256
EPSILON = 1e-05
HIGHEST_PRECISION = lax.Precision.HIGHEST


def from_behind(value, axis, steps):
    count = lax.axis_size(axis)
    first, last = (max(0, -steps), min(count, count - steps))
    return lax.ppermute(value, axis, [(source, source + steps) for source in range(first, last)])


def entering(part, axis, combine, identity):
    place = lax.axis_index(axis)
    gathered = jax.tree.map(lambda a: lax.all_gather(a, axis), part)
    state = jax.tree.map(lambda a, e: jnp.zeros_like(a) + jnp.asarray(e, a.dtype), part, identity)

    def one(step, state):
        return combine(
            state, jax.tree.map(lambda a: lax.dynamic_index_in_dim(a, step, 0, False), gathered)
        )

    return lax.fori_loop(0, place, one, state)


def conv_rows(prefix, raw_rows, kernel, shift_bias):
    row_count = raw_rows.shape[0]
    padded = jnp.concatenate([prefix, raw_rows], axis=0).astype(jnp.float32)
    summed = jnp.broadcast_to(shift_bias[None, :], raw_rows.shape)
    for tap_index in range(kernel.shape[0]):
        summed = summed + kernel[tap_index][None, :] * padded[tap_index : tap_index + row_count]
    return jax.nn.silu(summed).astype(jnp.bfloat16)


def shards(
    tokens,
    xz_weight,
    bc_weight,
    step_weight,
    step_bias,
    decay_log,
    skip_gain,
    conv_weight,
    conv_bias,
    bc_conv_weight,
    bc_conv_bias,
    norm_gain,
    step_bounds,
    readers,
):
    head_devices = lax.axis_size("heads")
    section = lax.axis_index("seq")
    head_block = lax.axis_index("heads")
    local_heads = H // head_devices
    per_group = H // G
    local_groups = max(1, local_heads // per_group)
    group_heads = local_heads // local_groups
    first_group = head_block * local_heads // per_group
    gathered = lax.all_gather(tokens, "heads", axis=1, tiled=True)
    row_count = gathered.shape[0]
    xz_rows = jnp.dot(
        gathered,
        lax.all_gather(xz_weight, "seq", axis=1, tiled=True),
        preferred_element_type=jnp.float32,
    ).astype(jnp.bfloat16)
    head_cols = xz_rows.reshape(row_count, local_heads, 2 * P_SIZE)
    inner_raw = head_cols[:, :, :P_SIZE].reshape(row_count, local_heads * P_SIZE)
    gate_raw = head_cols[:, :, P_SIZE:].reshape(row_count, local_groups, group_heads, P_SIZE)
    bc_part = jnp.dot(gathered, bc_weight, preferred_element_type=jnp.float32).astype(jnp.bfloat16)
    step_raw = jnp.dot(gathered, step_weight, preferred_element_type=jnp.float32)
    bc_every = lax.all_gather(bc_part, "heads", axis=1, tiled=True)
    width_bc = local_groups * 2 * N
    bc_mine = lax.dynamic_slice_in_dim(bc_every, first_group * 2 * N, width_bc, 1)
    kernel_bc = lax.dynamic_slice_in_dim(bc_conv_weight, first_group * 2 * N, width_bc, 1)
    shift_bc = lax.dynamic_slice_in_dim(bc_conv_bias, first_group * 2 * N, width_bc, 0)
    taps = conv_weight.shape[0]
    joined = jnp.concatenate([inner_raw, bc_mine], axis=1)
    previous = from_behind(joined[row_count - taps + 1 :], "seq", 1)
    inner_conv = conv_rows(
        previous[:, : local_heads * P_SIZE], inner_raw, conv_weight, conv_bias
    ).reshape(row_count, local_groups, group_heads, P_SIZE)
    bc_conv = conv_rows(previous[:, local_heads * P_SIZE :], bc_mine, kernel_bc, shift_bc).reshape(
        row_count, local_groups, 2 * N
    )
    b_input = bc_conv[:, :, :N]
    c_input = bc_conv[:, :, N:]
    step_size = jax.nn.softplus(step_raw + step_bias[None, :]).reshape(
        row_count, local_groups, group_heads
    )
    decay_rate = -jnp.exp(decay_log).reshape(local_groups, group_heads)[None] * step_size
    blocks = row_count // CH
    causal = lax.broadcasted_iota(jnp.int32, (CH, CH), 0) >= lax.broadcasted_iota(
        jnp.int32, (CH, CH), 1
    )
    running = jnp.zeros((local_groups, group_heads, P_SIZE, N), jnp.float32)
    local_starts = []
    intra_parts = []
    cum_parts = []
    block_totals = []
    for block_index in range(blocks):
        first_row = block_index * CH
        inner_blk = inner_conv[first_row : first_row + CH]
        b_blk = b_input[first_row : first_row + CH]
        c_blk = c_input[first_row : first_row + CH]
        step_blk = step_size[first_row : first_row + CH]
        cum_block = jnp.cumsum(decay_rate[first_row : first_row + CH], axis=0)
        scores = jnp.einsum("tgn,sgn->gts", c_blk, b_blk, preferred_element_type=jnp.float32)
        cum_gap = cum_block[:, None] - cum_block[None, :]
        weight = (
            jnp.where(causal[:, :, None, None], jnp.exp(jnp.minimum(cum_gap, 0.0)), 0.0)
            * step_blk[None]
        )
        mixing = (weight * jnp.transpose(scores, (1, 2, 0))[:, :, :, None]).astype(jnp.bfloat16)
        intra_parts.append(
            jnp.einsum("tsgr,sgrp->tgrp", mixing, inner_blk, preferred_element_type=jnp.float32)
        )
        cum_parts.append(cum_block)
        local_starts.append(running)
        block_total = cum_block[-1]
        block_totals.append(block_total)
        carry_weight = jnp.exp(block_total[None] - cum_block) * step_blk
        weighted = (inner_blk.astype(jnp.float32) * carry_weight[..., None]).astype(jnp.bfloat16)
        running = jnp.exp(block_total)[..., None, None] * running + jnp.einsum(
            "sgrp,sgn->grpn", weighted, b_blk, preferred_element_type=jnp.float32
        )
    section_decay = block_totals[0]
    block_index = 1
    section_decay = section_decay + block_totals[block_index]

    def combine(earlier, later):
        return (earlier[0] + later[0], jnp.exp(later[0])[..., None, None] * earlier[1] + later[1])

    identity = (jnp.zeros_like(section_decay), jnp.zeros_like(running))
    incoming = entering((section_decay, running), "seq", combine, identity)[1]
    global_starts = []
    ssd_parts = []
    prior_decay = jnp.zeros_like(section_decay)
    for block_index in range(blocks):
        start_state = local_starts[block_index] + jnp.exp(prior_decay)[..., None, None] * incoming
        global_starts.append(start_state)
        prior_decay = prior_decay + block_totals[block_index]
        first_row = block_index * CH
        c_blk = c_input[first_row : first_row + CH]
        outer_part = jnp.exp(cum_parts[block_index])[..., None] * jnp.einsum(
            "tgn,grpn->tgrp", c_blk.astype(jnp.float32), start_state, precision=HIGHEST_PRECISION
        )
        ssd_parts.append(intra_parts[block_index] + outer_part)
    ssd = jnp.concatenate(ssd_parts, axis=0) + skip_gain.reshape(local_groups, group_heads)[
        None, :, :, None
    ] * inner_conv.astype(jnp.float32)
    gated = ssd * jax.nn.silu(gate_raw.astype(jnp.float32))
    local_square = jnp.sum(gated * gated, axis=(2, 3))
    placed = lax.dynamic_update_slice_in_dim(
        jnp.zeros((row_count, G), jnp.float32), local_square, first_group, 1
    )
    square_total = lax.psum(placed, "heads")
    square_mean = lax.dynamic_slice_in_dim(square_total, first_group, local_groups, 1) / (
        per_group * P_SIZE
    )
    normed = (
        gated
        * lax.rsqrt(square_mean + EPSILON)[:, :, None, None]
        * norm_gain.reshape(local_groups, group_heads, P_SIZE)[None]
    )
    mixed = normed.astype(jnp.bfloat16).reshape(row_count, local_heads * P_SIZE)
    cum_all = jnp.concatenate(cum_parts, axis=0)
    starts_all = jnp.stack(global_starts, axis=0)
    positions = lax.broadcasted_iota(jnp.int32, (row_count,), 0)
    bound_local = (
        lax.dynamic_slice_in_dim(step_bounds, section * head_devices, head_devices, 0)
        - section * row_count
    )
    reader_local = lax.dynamic_slice_in_dim(readers, section * head_devices, head_devices, 0)
    block_of = bound_local // CH
    cum_at = cum_all[bound_local]
    inside_mask = (positions[None, :] // CH == block_of[:, None]) & (
        positions[None, :] <= bound_local[:, None]
    )
    cum_gap = cum_at[:, None] - cum_all[None]
    bound_weight = (
        jnp.where(inside_mask[:, :, None, None], jnp.exp(jnp.minimum(cum_gap, 0.0)), 0.0)
        * step_size[None]
    )
    bound_weighted = (inner_conv[None].astype(jnp.float32) * bound_weight[..., None]).astype(
        jnp.bfloat16
    )
    inside = jnp.einsum(
        "bsgrp,sgn->bgrpn", bound_weighted, b_input, preferred_element_type=jnp.float32
    )
    states = jnp.exp(cum_at)[..., None, None] * starts_all[block_of] + inside
    inverse = jnp.argsort(reader_local)
    ordered = states[inverse].reshape(head_devices, local_heads, P_SIZE, N).astype(jnp.bfloat16)
    arrived = lax.all_to_all(
        lax.all_to_all(ordered, "heads", split_axis=0, concat_axis=1, tiled=True),
        "seq",
        split_axis=1,
        concat_axis=0,
        tiled=True,
    )
    return (mixed, arrived[None])


def solution(mesh):
    in_specs = (
        P(("groups", "seq"), "heads"),
        P(None, ("heads", "seq")),
        P(None, "heads"),
        P(None, "heads"),
        P("heads"),
        P("heads"),
        P("heads"),
        P(None, "heads"),
        P("heads"),
        P(),
        P(),
        P("heads"),
        P("groups"),
        P("groups"),
    )
    out_specs = (P(("groups", "seq"), "heads"), P(("groups", "heads"), None, "seq", None, None))
    return jax.shard_map(shards, mesh=mesh, in_specs=in_specs, out_specs=out_specs, check_vma=False)
```

profile of v0, /device:TPU:6, one launch (start us, length us, event | category | flops | bytes accessed | tf_op | source)
XLA Modules:
  0.0 1422.9 jit_solution(13541814008040680989)
XLA Ops:
  8.0 152.5 %all-gather.6.cloned.1.call-done = bf16[512,8192]{1,0:T(8,128)(2,1)} async-done(((bf16[512,2048]{1,0:T(8,128)(2,1)}), bf16[512,8192]{1,0:T(8,128)(2,1)}) %all-gather.6.cloned.1.call-update) | async-done | bytes 8388624 | tf_op jit(solution)/shard_map/all_gather | solution.py:67
  160.4 11.0 convolution_convert_fusion.1
  174.6 6.4 compare_select_fusion
  185.7 30.3 %all-gather.10.cloned.1.call-done = bf16[512,2048]{1,0:T(8,128)(2,1)} async-done(((bf16[512,512]{1,0:T(8,128)(2,1)}), bf16[512,2048]{1,0:T(8,128)(2,1)}) %all-gather.10.cloned.1.call-update) | async-done | bytes 2097168 | tf_op jit(solution)/shard_map/all_gather | solution.py:79
  217.0 773.3 %all-gather.8.cloned.1.call-done = bf16[8192,8192]{1,0:T(8,128)(2,1)} async-done(((bf16[8192,2048]{1,0:T(8,128)(2,1)}), bf16[8192,8192]{1,0:T(8,128)(2,1)}) %all-gather.8.cloned.1.call-update) | async-done | bytes 134217744 | tf_op jit(solution)/shard_map/all_gather | solution.py:71
  990.3 79.7 %convolution_convert_fusion = bf16[512,8192]{1,0:T(8,128)(2,1)} fusion(bf16[512,8192]{1,0:T(8,128)(2,1)} %all-gather.6.cloned.1.call-done, bf16[8192,8192]{1,0:T(8,128)(2,1)} %all-gather.8.cloned.1.call-done), kind=kOutput, calls=%fused_computation.11 | convolution fusion | flops 68723671040 | bytes 150994944 | tf_op jit(solution)/shard_map/dot_general | solution.py:69
  1070.1 12.0 copy.125
  1082.1 7.6 slice_convert_fusion
  1089.6 6.3 copy.101
  1108.6 10.7 multiply_convert_fusion.6
  1127.3 5.1 all_gather.22
  1134.6 48.9 %all-gather.12.cloned.1.call-done = f32[8,32,64,128]{3,2,1,0:T(8,128)} async-done(((f32[2,32,64,128]{3,2,1,0:T(8,128)}), f32[8,32,64,128]{3,2,1,0:T(8,128)}) %all-gather.12.cloned.1.call-update) | async-done | bytes 8388624 | tf_op jit(solution)/shard_map/all_gather | solution.py:23
  1190.0 5.5 fusion.42
  1201.6 6.8 gather_fusion.1
  1208.5 7.2 fusion.31
  1215.8 6.8 fusion.32
  1222.7 14.6 %fusion.15 = (f32[512,2]{0,1:T(2,128)S(1)}, f32[512,4096]{0,1:T(8,128)}) fusion(f32[256,2,32,64]{0,3,2,1:T(8,128)S(1)} %fusion.31, f32[256,2,32,64]{0,3,2,1:T(8,128)} %fusion.32, f32[512,2,32,64]{0,3,2,1:T(8,128)} %bitcast.150, f32[2,32]{1,0:T(2,128)S(1)} %mul.366, f32[515,4096]{0,1:T(8,128)S(1)} %bitcast.147, f32[4096]{0:T(1024)S(1)} %bitcast.176, ...), kind=kLoop, calls=%fused_computation.30 | loop fusion | flops 50330624 | bytes 58806528 | tf_op jit(solution)/shard_map/reduce_sum | solution.py:160
  1237.3 9.6 bitcast_add_fusion.1
  1247.0 5.3 gather_fusion.2
  1252.3 99.6 %all_to_all.24 = bf16[4,64,64,128]{3,2,1,0:T(8,128)(2,1)} all-to-all(bf16[4,64,64,128]{3,2,1,0:T(8,128)(2,1)} %bitcast.155), channel_id=1, replica_groups=mesh['groups'=2,'seq'=4,'heads'=4] {'heads'}, dimensions={0} | all-to-all | bytes 8388608 | tf_op jit(solution)/shard_map/all_to_all | solution.py:202
  1357.0 17.2 %psum.7 = f32[512,8]{0,1:T(8,128)S(1)} all-reduce(f32[512,8]{0,1:T(8,128)S(1)} %dynamic_update_slice.3), channel_id=1, replica_groups=mesh['groups'=2,'seq'=4,'heads'=4] {'heads'}, use_global_device_ids=true, to_apply=%region_7.8 | all-reduce | flops 4096 | bytes 32768 | tf_op jit(solution)/shard_map/psum | solution.py:164
  1374.3 30.4 %fusion.12 = bf16[512,4096]{0,1:T(8,128)(2,1)} fusion(f32[256,4096]{0,1:T(8,128)} %bitcast.156, f32[256,4096]{0,1:T(8,128)} %bitcast.157, f32[512,64,64]{0,2,1:T(8,128)} %get-tuple-element.76, f32[4096]{0:T(1024)S(1)} %copy-done.29, f32[512,2]{0,1:T(2,128)S(1)} %add_rsqrt_fusion, f32[4096]{0:T(1024)S(1)} %mul.368, f32[515,4096]{0,1:T(8,128)} %copy-done.2, ...), kind=kLoop, calls=%fused_computation.26 | loop fusion | flops 52428800 | bytes 54644736 | tf_op jit(solution)/shard_map/convert_element_type | solution.py:173
  1404.6 6.3 copy.119
  1411.0 5.2 copy.181
  (168 shorter events, 53.7 us)
Async XLA Ops:
  7.2 167.3 %copy-start = (bf16[8192,64]{0,1:T(8,128)(2,1)S(1)}, bf16[8192,64]{0,1:T(8,128)(2,1)}, u32[]{:S(2)}) copy-start(bf16[8192,64]{0,1:T(8,128)(2,1)} %param.19) | copy-start | bytes 3145732
  7.2 153.3 %all-gather.6.cloned.1.call-start = ((), (), s32[]{:S(2)}) async-start(), calls=%async_computation.2 | async-start | bytes 10485760 | tf_op jit(solution)/shard_map/all_gather | solution.py:67
  7.9 208.0 %all-gather.10.cloned.1.call-start = ((), (), s32[]{:S(2)}) async-start(), calls=%async_computation.4 | async-start | bytes 2621440 | tf_op jit(solution)/shard_map/all_gather | solution.py:79
  171.5 818.8 %all-gather.8.cloned.1.call-start = ((), (), s32[]{:S(2)}) async-start(), calls=%async_computation.3 | async-start | bytes 167772160 | tf_op jit(solution)/shard_map/all_gather | solution.py:71
  172.3 1011.3 %all-gather.12.cloned.1.call-start = ((), (), s32[]{:S(2)}) async-start(), calls=%async_computation.5 | async-start | bytes 10485760 | tf_op jit(solution)/shard_map/all_gather | solution.py:23
  174.5 934.0 %copy-start.16 = (f32[1,4096]{1,0:T(1,128)}, f32[1,4096]{1,0:T(1,128)S(1)}, u32[]{:S(2)}) copy-start(f32[1,4096]{1,0:T(1,128)S(1)} %get-tuple-element.96) | copy-start | bytes 49156
  174.5 934.0 %copy-start.18 = (f32[1,4096]{1,0:T(1,128)}, f32[1,4096]{1,0:T(1,128)S(1)}, u32[]{:S(2)}) copy-start(f32[1,4096]{1,0:T(1,128)S(1)} %get-tuple-element.97) | copy-start | bytes 49156
  174.5 934.0 %copy-start.20 = (f32[1,4096]{1,0:T(1,128)}, f32[1,4096]{1,0:T(1,128)S(1)}, u32[]{:S(2)}) copy-start(f32[1,4096]{1,0:T(1,128)S(1)} %get-tuple-element.98) | copy-start | bytes 49156
  184.2 885.8 %copy-start.12 = (f32[256,64]{0,1:T(8,128)}, f32[256,64]{0,1:T(8,128)S(1)}, u32[]{:S(2)}) copy-start(f32[256,64]{0,1:T(8,128)S(1)} %get-tuple-element.85) | copy-start | bytes 196612
  184.3 885.8 %copy-start.14 = (f32[256,64]{0,1:T(8,128)}, f32[256,64]{0,1:T(8,128)S(1)}, u32[]{:S(2)}) copy-start(f32[256,64]{0,1:T(8,128)S(1)} %get-tuple-element.84) | copy-start | bytes 196612
  1096.8 5.3 collective-permute-start
  1100.1 21.6 %copy-start.27 = (f32[2,32]{1,0:T(2,128)}, f32[2,32]{1,0:T(2,128)S(1)}, u32[]{:S(2)}) copy-start(f32[2,32]{1,0:T(2,128)S(1)} %get-tuple-element.104) | copy-start | bytes 772
  1103.1 29.5 %copy-start.10 = (bf16[512,2,256]{2,1,0:T(2,128)(2,1)}, bf16[512,2,256]{2,1,0:T(2,128)(2,1)S(1)}, u32[]{:S(2)}) copy-start(bf16[512,2,256]{2,1,0:T(2,128)(2,1)S(1)} %reshape.225) | copy-start | bytes 1572868
  1108.5 10.8 copy-start.2
  1208.5 7.2 copy-start.6
  1208.5 7.2 copy-start.9
  1208.5 7.2 copy-start.11
  1208.5 7.2 copy-start.13
  1208.5 7.2 copy-start.25
  1215.7 7.0 copy-start.4
  1222.7 14.6 %slice-start.3 = ((bf16[512,2,256]{2,1,0:T(2,128)(2,1)}), bf16[512,2,128]{2,1,0:T(2,128)(2,1)S(1)}, s32[]{:S(2)}) async-start(bf16[512,2,256]{2,1,0:T(2,128)(2,1)} %copy-done.10), calls=%async_computation.9 | async-start | bytes 524288 | tf_op jit(solution)/shard_map/slice | solution.py:93
  1252.3 121.9 %copy-start.29 = (f32[4096]{0:T(1024)S(1)}, f32[4096]{0:T(1024)}, u32[]{:S(2)}) copy-start(f32[4096]{0:T(1024)} %param.27) | copy-start | bytes 49156
  1351.9 59.1 %all-to-all-start.1 = ((bf16[1,256,64,128]{3,2,0,1:T(8,128)(2,1)}), bf16[1,256,64,128]{3,2,0,1:T(8,128)(2,1)}, u32[]{:S(2)}, u32[]{:S(2)}) async-start(bf16[1,256,64,128]{3,2,0,1:T(8,128)(2,1)} %bitcast.154), calls=%async_computation.1 | async-start | bytes 8388608 | tf_op jit(solution)/shard_map/all_to_all | solution.py:201
  1374.2 41.9 %copy-start.1 = (bf16[8192,64]{0,1:T(8,128)(2,1)S(1)}, bf16[8192,64]{0,1:T(8,128)(2,1)}, u32[]{:S(2)}) copy-start(bf16[8192,64]{0,1:T(8,128)(2,1)} %param.19) | copy-start | bytes 3145732
  (22 other events, 111.7 us)
Sparse Core Ops, SparseCore 0:
  9.6 150.8 all-gather.5
  171.6 44.2 all-gather.9
  217.5 772.7 all-gather.7
  1125.2 58.2 all-gather.11
where the time goes:
time: 1430 us; the launch traced here: 1420 us
  waiting for transfers between devices  1010 us (71%)
  matrix products  135 us (9%)
  blocking collectives  122 us (9%)
  other arithmetic  83.8 us (6%)
  local copies, waits for them, and re-layouts  50.9 us (4%)
  between operations  14.8 us (1%)
    all_gather x1, waiting for transfers between devices, shards(): lax.all_gather(xz_weight, 'seq', axis=1, tiled=True)  773 us
    all_gather x1, waiting for transfers between devices, shards(): gathered = lax.all_gather(tokens, 'heads', axis=1, tiled=True)  152 us
    all_to_all x1, blocking collectives, shards(): lax.all_to_all(ordered, 'heads', split_axis=0, concat_axis=1, tiled=True)  99.6 us
    dot_general x1, matrix products, shards(): jnp.dot(gathered, lax.all_gather(xz_weight, 'seq', axis=1, tiled=True), p...  79.7 us
    all_gather x1, waiting for transfers between devices, entering(): gathered = jax.tree.map(lambda a: lax.all_gather(a, axis), part)  48.9 us
    convert_element_type x1, other arithmetic, shards(): mixed = normed.astype(jnp.bfloat16).reshape(row_count, local_heads * P_SIZE)  30.4 us
    all_gather x1, waiting for transfers between devices, shards(): bc_every = lax.all_gather(bc_part, 'heads', axis=1, tiled=True)  30.3 us
  transfers between devices with their start and end apart: 6, of which 5 were waited for; matrix products, arithmetic and copies ran while one was open for 4% of the time, Pallas kernels for 0%

commit v1 on v0

--- a/solution.py
+++ b/solution.py
@@ -198,13 +198,11 @@
     states = jnp.exp(cum_at)[..., None, None] * starts_all[block_of] + inside
     inverse = jnp.argsort(reader_local)
     ordered = states[inverse].reshape(head_devices, local_heads, P_SIZE, N).astype(jnp.bfloat16)
-    arrived = lax.all_to_all(
-        lax.all_to_all(ordered, "heads", split_axis=0, concat_axis=1, tiled=True),
-        "seq",
-        split_axis=1,
-        concat_axis=0,
-        tiled=True,
-    )
+    part_2 = lax.all_to_all(ordered, "heads", split_axis=0, concat_axis=1, tiled=True)
+    devices = lax.axis_size("seq")
+    pieces = jnp.stack(jnp.split(part_2, devices, axis=1), axis=0)
+    pieces = lax.all_to_all(pieces, "seq", split_axis=0, concat_axis=0)
+    arrived = jnp.concatenate(pieces, axis=0)
     return (mixed, arrived[None])
 
 

time: 1430 us -> 1430 us (level)
  no operation moved by 1% of the time
where the time goes in v1:
time: 1430 us
  waiting for transfers between devices  1010 us (71%)
  matrix products  135 us (9%)
  blocking collectives  121 us (8%)
  other arithmetic  86 us (6%)
  local copies, waits for them, and re-layouts  51.9 us (4%)
  between operations  14.8 us (1%)
    all_gather x1, waiting for transfers between devices, shards(): lax.all_gather(xz_weight, 'seq', axis=1, tiled=True)  773 us
    all_gather x1, waiting for transfers between devices, shards(): gathered = lax.all_gather(tokens, 'heads', axis=1, tiled=True)  152 us
    all_to_all x1, blocking collectives, shards(): lax.all_to_all(ordered, 'heads', split_axis=0, concat_axis=1, tiled=True)  98.4 us
    dot_general x1, matrix products, shards(): jnp.dot(gathered, lax.all_gather(xz_weight, 'seq', axis=1, tiled=True), p...  79.7 us
    all_gather x1, waiting for transfers between devices, entering(): gathered = jax.tree.map(lambda a: lax.all_gather(a, axis), part)  49 us
    convert_element_type x1, other arithmetic, shards(): mixed = normed.astype(jnp.bfloat16).reshape(row_count, local_heads * P_SIZE)  30.4 us
    all_gather x1, waiting for transfers between devices, shards(): bc_every = lax.all_gather(bc_part, 'heads', axis=1, tiled=True)  30.2 us
  transfers between devices with their start and end apart: 6, of which 5 were waited for; matrix products, arithmetic and copies ran while one was open for 4% of the time, Pallas kernels for 0%

profile of v1, /device:TPU:6, one launch (start us, length us, event | category | flops | bytes accessed | tf_op | source)
XLA Modules:
  0.0 1425.0 jit_solution(5924007737416059437)
XLA Ops:
  8.0 152.5 %all-gather.6.cloned.1.call-done = bf16[512,8192]{1,0:T(8,128)(2,1)} async-done(((bf16[512,2048]{1,0:T(8,128)(2,1)}), bf16[512,8192]{1,0:T(8,128)(2,1)}) %all-gather.6.cloned.1.call-update) | async-done | bytes 8388624 | tf_op jit(solution)/shard_map/all_gather | solution.py:67
  160.4 11.0 convolution_convert_fusion.1
  174.6 6.4 compare_select_fusion
  185.7 30.2 %all-gather.10.cloned.1.call-done = bf16[512,2048]{1,0:T(8,128)(2,1)} async-done(((bf16[512,512]{1,0:T(8,128)(2,1)}), bf16[512,2048]{1,0:T(8,128)(2,1)}) %all-gather.10.cloned.1.call-update) | async-done | bytes 2097168 | tf_op jit(solution)/shard_map/all_gather | solution.py:79
  217.0 773.3 %all-gather.8.cloned.1.call-done = bf16[8192,8192]{1,0:T(8,128)(2,1)} async-done(((bf16[8192,2048]{1,0:T(8,128)(2,1)}), bf16[8192,8192]{1,0:T(8,128)(2,1)}) %all-gather.8.cloned.1.call-update) | async-done | bytes 134217744 | tf_op jit(solution)/shard_map/all_gather | solution.py:71
  990.3 79.7 %convolution_convert_fusion = bf16[512,8192]{1,0:T(8,128)(2,1)} fusion(bf16[512,8192]{1,0:T(8,128)(2,1)} %all-gather.6.cloned.1.call-done, bf16[8192,8192]{1,0:T(8,128)(2,1)} %all-gather.8.cloned.1.call-done), kind=kOutput, calls=%fused_computation.11 | convolution fusion | flops 68723671040 | bytes 150994944 | tf_op jit(solution)/shard_map/dot_general | solution.py:69
  1070.1 12.0 copy.134
  1082.1 7.6 slice_convert_fusion
  1089.6 6.3 copy.110
  1108.6 10.7 multiply_convert_fusion.6
  1127.2 5.1 all_gather.22
  1134.5 49.0 %all-gather.12.cloned.1.call-done = f32[8,32,64,128]{3,2,1,0:T(8,128)} async-done(((f32[2,32,64,128]{3,2,1,0:T(8,128)}), f32[8,32,64,128]{3,2,1,0:T(8,128)}) %all-gather.12.cloned.1.call-update) | async-done | bytes 8388624 | tf_op jit(solution)/shard_map/all_gather | solution.py:23
  1190.0 5.5 fusion.42
  1201.7 6.8 gather_fusion.1
  1208.5 7.2 fusion.31
  1215.8 6.8 fusion.32
  1222.8 14.6 %fusion.15 = (f32[512,2]{0,1:T(2,128)S(1)}, f32[512,4096]{0,1:T(8,128)}) fusion(f32[256,2,32,64]{0,3,2,1:T(8,128)S(1)} %fusion.31, f32[256,2,32,64]{0,3,2,1:T(8,128)} %fusion.32, f32[512,2,32,64]{0,3,2,1:T(8,128)} %bitcast.158, f32[2,32]{1,0:T(2,128)S(1)} %mul.366, f32[515,4096]{0,1:T(8,128)S(1)} %bitcast.155, f32[4096]{0:T(1024)S(1)} %bitcast.184, ...), kind=kLoop, calls=%fused_computation.30 | loop fusion | flops 50330624 | bytes 58806528 | tf_op jit(solution)/shard_map/reduce_sum | solution.py:160
  1237.4 9.6 bitcast_add_fusion.1
  1247.0 5.3 gather_fusion.2
  1252.3 98.4 %all_to_all.17 = bf16[4,64,64,128]{3,2,1,0:T(8,128)(2,1)S(1)} all-to-all(bf16[4,64,64,128]{3,2,1,0:T(8,128)(2,1)} %bitcast.163), channel_id=1, replica_groups=mesh['groups'=2,'seq'=4,'heads'=4] {'heads'}, dimensions={0} | all-to-all | bytes 8388608 | tf_op jit(solution)/shard_map/all_to_all | solution.py:201
  1359.2 17.2 %psum.7 = f32[512,8]{0,1:T(8,128)S(1)} all-reduce(f32[512,8]{0,1:T(8,128)S(1)} %dynamic_update_slice.3), channel_id=1, replica_groups=mesh['groups'=2,'seq'=4,'heads'=4] {'heads'}, use_global_device_ids=true, to_apply=%region_7.8 | all-reduce | flops 4096 | bytes 32768 | tf_op jit(solution)/shard_map/psum | solution.py:164
  1376.4 30.4 %fusion.12 = bf16[512,4096]{0,1:T(8,128)(2,1)} fusion(f32[256,4096]{0,1:T(8,128)} %bitcast.164, f32[256,4096]{0,1:T(8,128)} %bitcast.165, f32[512,64,64]{0,2,1:T(8,128)} %get-tuple-element.76, f32[4096]{0:T(1024)S(1)} %copy-done.29, f32[512,2]{0,1:T(2,128)S(1)} %add_rsqrt_fusion, f32[4096]{0:T(1024)S(1)} %mul.368, f32[515,4096]{0,1:T(8,128)} %copy-done.2, ...), kind=kLoop, calls=%fused_computation.26 | loop fusion | flops 52428800 | bytes 54644736 | tf_op jit(solution)/shard_map/convert_element_type | solution.py:173
  1406.8 6.3 copy.128
  1413.1 5.2 copy.190
  (174 shorter events, 57.0 us)
Async XLA Ops:
  7.2 167.3 %copy-start = (bf16[8192,64]{0,1:T(8,128)(2,1)S(1)}, bf16[8192,64]{0,1:T(8,128)(2,1)}, u32[]{:S(2)}) copy-start(bf16[8192,64]{0,1:T(8,128)(2,1)} %param.19) | copy-start | bytes 3145732
  7.2 153.3 %all-gather.6.cloned.1.call-start = ((), (), s32[]{:S(2)}) async-start(), calls=%async_computation.2 | async-start | bytes 10485760 | tf_op jit(solution)/shard_map/all_gather | solution.py:67
  7.9 208.0 %all-gather.10.cloned.1.call-start = ((), (), s32[]{:S(2)}) async-start(), calls=%async_computation.4 | async-start | bytes 2621440 | tf_op jit(solution)/shard_map/all_gather | solution.py:79
  171.5 818.8 %all-gather.8.cloned.1.call-start = ((), (), s32[]{:S(2)}) async-start(), calls=%async_computation.3 | async-start | bytes 167772160 | tf_op jit(solution)/shard_map/all_gather | solution.py:71
  172.3 1011.3 %all-gather.12.cloned.1.call-start = ((), (), s32[]{:S(2)}) async-start(), calls=%async_computation.5 | async-start | bytes 10485760 | tf_op jit(solution)/shard_map/all_gather | solution.py:23
  174.5 934.0 %copy-start.16 = (f32[1,4096]{1,0:T(1,128)}, f32[1,4096]{1,0:T(1,128)S(1)}, u32[]{:S(2)}) copy-start(f32[1,4096]{1,0:T(1,128)S(1)} %get-tuple-element.100) | copy-start | bytes 49156
  174.5 934.0 %copy-start.18 = (f32[1,4096]{1,0:T(1,128)}, f32[1,4096]{1,0:T(1,128)S(1)}, u32[]{:S(2)}) copy-start(f32[1,4096]{1,0:T(1,128)S(1)} %get-tuple-element.101) | copy-start | bytes 49156
  174.5 934.0 %copy-start.20 = (f32[1,4096]{1,0:T(1,128)}, f32[1,4096]{1,0:T(1,128)S(1)}, u32[]{:S(2)}) copy-start(f32[1,4096]{1,0:T(1,128)S(1)} %get-tuple-element.102) | copy-start | bytes 49156
  184.2 885.8 %copy-start.12 = (f32[256,64]{0,1:T(8,128)}, f32[256,64]{0,1:T(8,128)S(1)}, u32[]{:S(2)}) copy-start(f32[256,64]{0,1:T(8,128)S(1)} %get-tuple-element.89) | copy-start | bytes 196612
  184.3 885.8 %copy-start.14 = (f32[256,64]{0,1:T(8,128)}, f32[256,64]{0,1:T(8,128)S(1)}, u32[]{:S(2)}) copy-start(f32[256,64]{0,1:T(8,128)S(1)} %get-tuple-element.88) | copy-start | bytes 196612
  1096.8 5.3 collective-permute-start
  1100.1 21.6 %copy-start.27 = (f32[2,32]{1,0:T(2,128)}, f32[2,32]{1,0:T(2,128)S(1)}, u32[]{:S(2)}) copy-start(f32[2,32]{1,0:T(2,128)S(1)} %get-tuple-element.108) | copy-start | bytes 772
  1103.1 29.4 %copy-start.10 = (bf16[512,2,256]{2,1,0:T(2,128)(2,1)}, bf16[512,2,256]{2,1,0:T(2,128)(2,1)S(1)}, u32[]{:S(2)}) copy-start(bf16[512,2,256]{2,1,0:T(2,128)(2,1)S(1)} %reshape.222) | copy-start | bytes 1572868
  1108.6 10.8 copy-start.2
  1125.2 97.4 %copy-start.32 = (f32[2,32]{1,0:T(2,128)}, f32[2,32]{1,0:T(2,128)S(1)}, u32[]{:S(2)}) copy-start(f32[2,32]{1,0:T(2,128)S(1)} %mul.366) | copy-start | bytes 772
  1208.5 7.2 copy-start.6
  1208.5 7.2 copy-start.9
  1208.5 7.2 copy-start.11
  1208.5 7.2 copy-start.13
  1208.5 7.2 copy-start.25
  1222.7 14.6 %slice-start.3 = ((bf16[512,2,256]{2,1,0:T(2,128)(2,1)}), bf16[512,2,128]{2,1,0:T(2,128)(2,1)S(1)}, s32[]{:S(2)}) async-start(bf16[512,2,256]{2,1,0:T(2,128)(2,1)} %copy-done.10), calls=%async_computation.9 | async-start | bytes 524288 | tf_op jit(solution)/shard_map/slice | solution.py:93
  1351.7 24.7 %copy-start.29 = (f32[4096]{0:T(1024)S(1)}, f32[4096]{0:T(1024)}, u32[]{:S(2)}) copy-start(f32[4096]{0:T(1024)} %param.27) | copy-start | bytes 49156
  1354.0 59.1 %all-to-all-start.1 = ((bf16[4,1,64,64,128]{4,3,2,1,0:T(8,128)(2,1)}), bf16[4,1,64,64,128]{4,3,2,1,0:T(8,128)(2,1)}, u32[]{:S(2)}, u32[]{:S(2)}) async-start(bf16[4,1,64,64,128]{4,3,2,1,0:T(8,128)(2,1)} %pad_maximum_fusion.1), calls=%async_computation.1 | async-start | bytes 8388608 | tf_op jit(solution)/shard_map/all_to_all | solution.py:204
  1376.4 41.9 %copy-start.1 = (bf16[8192,64]{0,1:T(8,128)(2,1)S(1)}, bf16[8192,64]{0,1:T(8,128)(2,1)}, u32[]{:S(2)}) copy-start(bf16[8192,64]{0,1:T(8,128)(2,1)} %param.19) | copy-start | bytes 3145732
  (24 other events, 125.9 us)
Sparse Core Ops, SparseCore 0:
  9.6 150.8 all-gather.5
  171.6 44.2 all-gather.9
  217.5 772.7 all-gather.7
  1125.3 58.2 all-gather.11
